TPU v7x, 256 devices: a whole 4x4x8 slice. The times are simulated.
256 devices in a mesh: row: 16 (over y, x), col: 16 (over z, core).
Axes of the slice: x: 4, y: 4, z: 8, core: 2. Of those that a mesh axis runs over, the one named last changes fastest.
Arguments:
- hidden_in: bfloat16 [1024, 4096], P('col', 'row'), may hold values from -250 to 250
- norm_gain: bfloat16 [4096], P('row'), may hold values from 0.099609375 to 1.8984375
- w_qkv: bfloat16 [4096, 6144], P('row', 'col'), may hold values from -0.125 to 0.125
- w_out: bfloat16 [4096, 4096], P('row', 'col'), may hold values from -0.125 to 0.125
- cache_k: bfloat16 [16, 4096, 1024], P('col', 'row'), may hold values from -1300 to 1300
- value_cache: bfloat16 [16, 4096, 1024], P('col', 'row'), may hold values from -6 to 6
- cache_len: int32 [16], P('col'), may hold values from 1 to 4096, as said below
- parents: int32 [16, 64], P('col'), may hold values from -1 to 62, as said below
Outputs:
- update: bfloat16 [1024, 4096], P('col', 'row')
Inputs may be any that keep to these rules, and one draw needn't show every extreme that they name: Slots 0 to cache_len - 1 of a request's window are filled; some request fills all 4096 slots. `parents`: slot 0 of every request is the root with parent -1; every other slot's parent is an earlier slot of the same request; slot 63 has parent 64 - 2.
All inputs are finite; a program needn't handle non-finite values.
Results may differ from a plain program's by a relative error of at most 0.011.
The roundings to bfloat16 on the way count: a program that leaves them out, or rounds other values in their place, can miss the bound.
Values may be sent and summed in bfloat16 or wider, within the bound.
A program may use at most 128 MiB of HBM per device.

v0:
```python
import jax
import jax.numpy as jnp
from jax import lax
from jax.sharding import PartitionSpec as P

D = 4096
QUERY_HEADS = 32
KEY_VALUE_HEADS = 8
HEAD_SIZE = 128
masked_score = -1e30


def ancestors(parents):
    draft_tree = parents.shape[1]
    slot_ids = jnp.arange(draft_tree, dtype=jnp.int32)
    parent_links = (parents[:, :, None] == slot_ids[None, None, :]).astype(jnp.float32)
    reachable = parent_links + jnp.eye(draft_tree, dtype=jnp.float32)[None]
    for squaring in range(max(1, (draft_tree - 1).bit_length())):
        product = jnp.einsum("rij,rjk->rik", reachable, reachable, precision=lax.Precision.HIGHEST)
        reachable = (product > 0.5).astype(jnp.float32)
    return reachable > 0.5


def row_reduce(partial, axis_name, sent=jnp.float32):
    count = lax.axis_size(axis_name)
    rows, cols = partial.shape
    pieces = partial.reshape(rows, count, cols // count).transpose(1, 0, 2).astype(sent)
    received = lax.all_to_all(pieces, axis_name, 0, 0)
    return jnp.sum(received.astype(jnp.float32), axis=0)


def row_gather(value, axis_name):
    count = lax.axis_size(axis_name)
    copies = jnp.broadcast_to(value[None], (count,) + value.shape)
    return lax.all_to_all(copies, axis_name, 0, 0)


def shards(hidden_in, norm_gain, w_qkv, w_out, cache_k, value_cache, cache_len, parents):
    rows_here = hidden_in.shape[0]
    request_list = cache_k.shape[0]
    token_positions = cache_k.shape[1]
    draft_tree = parents.shape[1]
    head_groups = QUERY_HEADS // KEY_VALUE_HEADS
    row_count = lax.axis_size("row")
    heads_dev = QUERY_HEADS // row_count
    row_index = lax.axis_index("row")
    score_scale = HEAD_SIZE ** (-0.5)
    features = hidden_in.astype(jnp.float32)
    squares = jnp.sum(row_gather(jnp.sum(features * features, axis=1), "row"), axis=0)
    row_scale = lax.rsqrt(squares / D + 1e-05)
    normed = (features * row_scale[:, None] * norm_gain.astype(jnp.float32)[None, :]).astype(
        jnp.bfloat16
    )
    half = w_qkv.shape[1] // 2
    halves = []
    for part in (w_qkv[:, :half], w_qkv[:, half:]):
        partial_value = jnp.dot(
            normed,
            lax.all_gather(part, "col", axis=1, tiled=True),
            preferred_element_type=jnp.float32,
        )
        halves.append(row_reduce(partial_value, "row"))
    summed = jnp.concatenate(halves, axis=1).astype(jnp.bfloat16)
    projected_output = row_gather(summed, "row").transpose(1, 0, 2).reshape(rows_here, -1)
    query_block = projected_output[:, : QUERY_HEADS * HEAD_SIZE].reshape(
        request_list, draft_tree, KEY_VALUE_HEADS, head_groups, HEAD_SIZE
    )
    new_key_block = projected_output[
        :, QUERY_HEADS * HEAD_SIZE : (QUERY_HEADS + KEY_VALUE_HEADS) * HEAD_SIZE
    ].reshape(request_list, draft_tree, KEY_VALUE_HEADS, HEAD_SIZE)
    new_value_block = projected_output[:, (QUERY_HEADS + KEY_VALUE_HEADS) * HEAD_SIZE :].reshape(
        request_list, draft_tree, KEY_VALUE_HEADS, HEAD_SIZE
    )
    first_slot = row_index * token_positions
    slot_ids = first_slot + jnp.arange(token_positions, dtype=jnp.int32)

    def cache_part(request_item):
        query_rows, cached_key_rows, cached_value_rows, length = request_item
        key_row_block = cached_key_rows.reshape(token_positions, KEY_VALUE_HEADS, HEAD_SIZE)
        value_row_block = cached_value_rows.reshape(token_positions, KEY_VALUE_HEADS, HEAD_SIZE)
        scores = (
            jnp.einsum(
                "tkgd,pkd->kgtp", query_rows, key_row_block, preferred_element_type=jnp.float32
            )
            * score_scale
        )
        visible = (slot_ids < length)[None, None, None, :]
        scores = jnp.where(visible, scores, masked_score)
        highest = jnp.max(scores, axis=-1)
        weights = jnp.where(visible, jnp.exp(scores - highest[..., None]), 0.0)
        totals = jnp.sum(weights, axis=-1)
        blended = jnp.einsum(
            "kgtp,pkd->kgtd",
            weights.astype(jnp.bfloat16),
            value_row_block,
            preferred_element_type=jnp.float32,
        )
        stats = jnp.concatenate(
            [highest.reshape(QUERY_HEADS, draft_tree), totals.reshape(QUERY_HEADS, draft_tree)],
            axis=-1,
        )
        return jnp.concatenate(
            [blended.reshape(QUERY_HEADS, draft_tree, HEAD_SIZE), stats[:, None, :]], axis=1
        )

    packed = lax.map(cache_part, (query_block, cache_k, value_cache, cache_len))
    packed = packed.reshape(request_list, row_count, heads_dev, draft_tree + 1, HEAD_SIZE)
    gathered = lax.all_to_all(packed, "row", 1, 1)
    block_blend = gathered[:, :, :, :draft_tree, :]
    block_max = gathered[:, :, :, draft_tree, :draft_tree]
    block_total = gathered[:, :, :, draft_tree, draft_tree : 2 * draft_tree]
    allowed = ancestors(parents)[:, None, :, :]
    query_heads = projected_output[:, : QUERY_HEADS * HEAD_SIZE].reshape(
        request_list, draft_tree, QUERY_HEADS, HEAD_SIZE
    )
    query_own = lax.dynamic_slice_in_dim(query_heads, row_index * heads_dev, heads_dev, 2)
    key_own = lax.dynamic_slice_in_dim(
        jnp.repeat(new_key_block, head_groups, axis=2), row_index * heads_dev, heads_dev, 2
    )
    value_own = lax.dynamic_slice_in_dim(
        jnp.repeat(new_value_block, head_groups, axis=2), row_index * heads_dev, heads_dev, 2
    )
    tree_scores = (
        jnp.einsum("rthd,rshd->rhts", query_own, key_own, preferred_element_type=jnp.float32)
        * score_scale
    )
    tree_scores = jnp.where(allowed, tree_scores, masked_score)
    tree_max = jnp.max(tree_scores, axis=-1)
    tree_weights = jnp.where(allowed, jnp.exp(tree_scores - tree_max[..., None]), 0.0)
    tree_total = jnp.sum(tree_weights, axis=-1)
    tree_blend = jnp.einsum(
        "rhts,rshd->rhtd",
        tree_weights.astype(jnp.bfloat16),
        value_own,
        preferred_element_type=jnp.float32,
    )
    joint_max = jnp.maximum(jnp.max(block_max, axis=1), tree_max)
    block_scale = jnp.exp(block_max - joint_max[:, None])
    tree_scale = jnp.exp(tree_max - joint_max)
    numerator = (
        jnp.sum(block_blend * block_scale[..., None], axis=1) + tree_blend * tree_scale[..., None]
    )
    denominator = jnp.sum(block_total * block_scale, axis=1) + tree_total * tree_scale
    attended = (numerator / denominator[..., None]).astype(jnp.bfloat16)
    attended = attended.transpose(0, 2, 1, 3).reshape(rows_here, heads_dev * HEAD_SIZE)
    partial_out = jnp.dot(
        attended,
        lax.all_gather(w_out, "col", axis=1, tiled=True),
        preferred_element_type=jnp.float32,
    )
    return row_reduce(partial_out, "row", jnp.bfloat16).astype(jnp.bfloat16)


def solution(mesh):
    placed = (
        P("col", "row"),
        P("row"),
        P("row", "col"),
        P("row", "col"),
        P("col", "row", None),
        P("col", "row", None),
        P("col"),
        P("col", None),
    )
    return jax.shard_map(
        shards, mesh=mesh, in_specs=placed, out_specs=P("col", "row"), check_vma=False
    )
```

profile of v0, /device:TPU:1, one launch (start us, length us, event | category | flops | bytes accessed | tf_op | source)
XLA Modules:
  0.0 190.4 jit_solution(11534638111007706878)
XLA Ops:
  6.5 1.1 fusion.53
  7.6 0.7 copy.112
  8.4 0.7 copy.111
  9.2 0.9 fusion.25
  10.1 0.6 broadcast_in_dim.88
  10.7 7.6 %all-to-all-start = ((f32[16,1,64]{2,1,0:T(1,128)}), f32[16,1,64]{2,1,0:T(1,128)S(1)}, u32[]{:S(2)}, u32[]{:S(2)}) async-start(f32[16,1,64]{2,1,0:T(1,128)} %broadcast_in_dim.88), calls=%async_computation | async-start | bytes 16384 | tf_op jit(solution)/shard_map/all_to_all | solution.py:35
  18.3 0.7 all-gather.8.cloned.1.call-update
  19.0 0.7 convert_element_type.93
  19.7 5.0 %all-to-all-done = f32[16,1,64]{2,1,0:T(1,128)S(1)} async-done(((f32[16,1,64]{2,1,0:T(1,128)}), f32[16,1,64]{2,1,0:T(1,128)S(1)}, u32[]{:S(2)}, u32[]{:S(2)}) %all-to-all-start) | async-done | bytes 4128 | tf_op jit(solution)/shard_map/all_to_all | solution.py:35
  24.7 27.6 %all-gather.6.cloned.1.call-done = bf16[256,3072]{0,1:T(8,128)(2,1)} async-done(((bf16[256,192]{0,1:T(8,128)(2,1)}), bf16[256,3072]{0,1:T(8,128)(2,1)}) %all-gather.6.cloned.1.call-update) | async-done | bytes 1572880 | tf_op jit(solution)/shard_map/all_gather | solution.py:59
  52.3 2.0 %fusion.43 = f32[64,3072]{1,0:T(8,128)S(1)} fusion(bf16[256,3072]{0,1:T(8,128)(2,1)} %all-gather.6.cloned.1.call-done, bf16[64,256]{1,0:T(8,128)(2,1)} %param.8, f32[256]{0:T(256)S(1)} %convert_element_type.93, f32[64]{0:T(128)S(1)} %add_rsqrt_fusion), kind=kOutput, calls=%fused_computation.71 | convolution fusion | flops 100728832 | bytes 2393344 | tf_op jit(solution)/shard_map/dot_general | solution.py:57
  54.3 0.5 reshape.367
  54.8 1.6 copy.141
  56.4 6.6 %all-to-all-start.2 = ((f32[16,64,192]{2,1,0:T(8,128)}), f32[16,64,192]{2,1,0:T(8,128)S(1)}, u32[]{:S(2)}, u32[]{:S(2)}) async-start(f32[16,64,192]{2,1,0:T(8,128)} %bitcast.99), calls=%async_computation.2 | async-start | bytes 2097152 | tf_op jit(solution)/shard_map/all_to_all | solution.py:28
  63.0 28.7 %all-gather.4.cloned.1.call-done = bf16[256,3072]{0,1:T(8,128)(2,1)} async-done(((bf16[256,192]{0,1:T(8,128)(2,1)}), bf16[256,3072]{0,1:T(8,128)(2,1)}) %all-gather.4.cloned.1.call-update) | async-done | bytes 1572880 | tf_op jit(solution)/shard_map/all_gather | solution.py:59
  91.7 2.0 %fusion.45 = f32[64,3072]{1,0:T(8,128)S(1)} fusion(bf16[256,3072]{0,1:T(8,128)(2,1)} %all-gather.4.cloned.1.call-done, bf16[64,256]{1,0:T(8,128)(2,1)S(1)} %copy-done.4, f32[256]{0:T(256)S(1)} %convert_element_type.93, f32[64]{0:T(128)S(1)} %add_rsqrt_fusion), kind=kOutput, calls=%fused_computation.72 | convolution fusion | flops 100728832 | bytes 2393344 | tf_op jit(solution)/shard_map/dot_general | solution.py:57
  93.7 0.5 reshape.366
  94.2 1.6 copy.142
  95.8 6.7 %all-to-all-start.1 = ((f32[16,64,192]{2,1,0:T(8,128)}), f32[16,64,192]{2,1,0:T(8,128)S(1)}, u32[]{:S(2)}, u32[]{:S(2)}) async-start(f32[16,64,192]{2,1,0:T(8,128)} %bitcast.100), calls=%async_computation.1 | async-start | bytes 2097152 | tf_op jit(solution)/shard_map/all_to_all | solution.py:28
  103.1 0.9 copy.117
  104.2 0.1 fusion.31
  104.4 14.5 %all-to-all-done.1 = f32[16,64,192]{2,1,0:T(8,128)S(1)} async-done(((f32[16,64,192]{2,1,0:T(8,128)}), f32[16,64,192]{2,1,0:T(8,128)S(1)}, u32[]{:S(2)}, u32[]{:S(2)}) %all-to-all-start.1) | async-done | bytes 786464 | tf_op jit(solution)/shard_map/all_to_all | solution.py:28
  119.1 1.0 broadcast_in_dim.89
  120.1 4.5 %all-to-all-start.3 = ((bf16[16,64,384]{2,1,0:T(8,128)(2,1)}), bf16[16,64,384]{2,1,0:T(8,128)(2,1)S(1)}, u32[]{:S(2)}, u32[]{:S(2)}) async-start(bf16[16,64,384]{2,1,0:T(8,128)(2,1)} %broadcast_in_dim.89), calls=%async_computation.3 | async-start | bytes 1572864 | tf_op jit(solution)/shard_map/all_to_all | solution.py:35
  124.6 0.2 convolution_compare_fusion.5
  125.0 0.1 convolution_compare_fusion.2
  125.2 0.1 convolution_compare_fusion.1
  125.3 12.4 %all-to-all-done.3 = bf16[16,64,384]{2,1,0:T(8,128)(2,1)S(1)} async-done(((bf16[16,64,384]{2,1,0:T(8,128)(2,1)}), bf16[16,64,384]{2,1,0:T(8,128)(2,1)S(1)}, u32[]{:S(2)}, u32[]{:S(2)}) %all-to-all-start.3) | async-done | bytes 786464 | tf_op jit(solution)/shard_map/all_to_all | solution.py:35
  137.8 0.9 copy-done
  138.7 1.0 slice_bitcast_fusion.3
  139.6 0.4 squeeze.24
  140.0 0.6 bitcast_reduce_fusion
  140.6 0.7 fusion.12
  141.3 0.8 copy.93
  142.1 0.9 fusion.2
  143.1 1.5 maximum_maximum_fusion
  144.6 3.9 %all-to-all-start.4 = ((f32[1,16,2,65,128]{4,2,3,0,1:T(2,128)}), f32[1,16,2,65,128]{4,2,3,0,1:T(2,128)S(1)}, u32[]{:S(2)}, u32[]{:S(2)}) async-start(f32[1,16,2,65,128]{4,2,3,0,1:T(2,128)} %maximum_maximum_fusion), calls=%async_computation.4 | async-start | bytes 2129920 | tf_op jit(solution)/shard_map/all_to_all | solution.py:108
  148.8 3.3 %copy.103 = bf16[4096,256]{1,0:T(8,128)(2,1)S(1)} copy(bf16[4096,256]{0,1:T(8,128)(2,1)} %bitcast.106) | data formatting | bytes 4194304 | tf_op jit(solution)/shard_map/dot_general | solution.py:146
  152.0 1.1 copy.119
  153.2 1.0 slice_bitcast_fusion
  154.4 0.2 fusion.54
  154.6 9.1 %all-to-all-done.4 = f32[1,16,2,65,128]{4,2,3,0,1:T(2,128)S(1)} async-done(((f32[1,16,2,65,128]{4,2,3,0,1:T(2,128)}), f32[1,16,2,65,128]{4,2,3,0,1:T(2,128)S(1)}, u32[]{:S(2)}, u32[]{:S(2)}) %all-to-all-start.4) | async-done | bytes 1064992 | tf_op jit(solution)/shard_map/all_to_all | solution.py:108
  163.8 1.0 copy.98
  164.9 2.2 %fusion.14 = f32[2,64,128]{2,0,1:T(2,128)S(1)} fusion(f32[1,16,2,65,128]{4,2,3,0,1:T(2,128)S(1)} %all-to-all-done.4, f32[16,2,64]{1,2,0:T(8,128)} %copy.98), kind=kLoop, calls=%fused_computation.27 | loop fusion | flops 507904 | bytes 1122304 | tf_op jit(solution)/shard_map/reduce_sum | solution.py:141
  167.3 0.2 fusion.9
  167.6 0.7 fusion.4
  168.4 14.8 %all_to_all.31 = bf16[16,64,256]{2,1,0:T(8,128)(2,1)S(1)} all-to-all(bf16[16,64,256]{2,1,0:T(8,128)(2,1)S(1)} %fusion.4), channel_id=1, replica_groups=mesh['row'=16,'col'=16] {'row'}, dimensions={0} | all-to-all | bytes 1048576 | tf_op jit(solution)/shard_map/all_to_all | solution.py:28
  183.2 0.7 reduce_sum.93
  (42 shorter events, 1.7 us)
Async XLA Ops:
  6.5 45.7 %all-gather.6.cloned.1.call-start = ((), (), s32[]{:S(2)}) async-start(), calls=%async_computation.7 | async-start | bytes 1671168 | tf_op jit(solution)/shard_map/all_gather | solution.py:59
  8.4 83.3 %all-gather.4.cloned.1.call-start = ((), (), s32[]{:S(2)}) async-start(), calls=%async_computation.6 | async-start | bytes 1671168 | tf_op jit(solution)/shard_map/all_gather | solution.py:59
  10.7 13.9 %all-to-all-start = ((f32[16,1,64]{2,1,0:T(1,128)}), f32[16,1,64]{2,1,0:T(1,128)S(1)}, u32[]{:S(2)}, u32[]{:S(2)}) async-start(f32[16,1,64]{2,1,0:T(1,128)} %broadcast_in_dim.88), calls=%async_computation | async-start | bytes 16384 | tf_op jit(solution)/shard_map/all_to_all | solution.py:35
  18.3 130.5 %all-gather.8.cloned.1.call-start = ((), (), s32[]{:S(2)}) async-start(), calls=%async_computation.8 | async-start | bytes 2228224 | tf_op jit(solution)/shard_map/all_gather | solution.py:148
  54.8 36.9 %copy-start.4 = (bf16[64,256]{1,0:T(8,128)(2,1)S(1)}, bf16[64,256]{1,0:T(8,128)(2,1)}, u32[]{:S(2)}) copy-start(bf16[64,256]{1,0:T(8,128)(2,1)} %param.8) | copy-start | bytes 98308
  56.4 39.5 %all-to-all-start.2 = ((f32[16,64,192]{2,1,0:T(8,128)}), f32[16,64,192]{2,1,0:T(8,128)S(1)}, u32[]{:S(2)}, u32[]{:S(2)}) async-start(f32[16,64,192]{2,1,0:T(8,128)} %bitcast.99), calls=%async_computation.2 | async-start | bytes 2097152 | tf_op jit(solution)/shard_map/all_to_all | solution.py:28
  94.2 8.9 %copy-start.1 = (bf16[1,256,1024]{2,1,0:T(8,128)(2,1)S(1)}, bf16[1,256,1024]{2,1,0:T(8,128)(2,1)}, u32[]{:S(2)}) copy-start(bf16[1,256,1024]{2,1,0:T(8,128)(2,1)} %param.12) | copy-start | bytes 1572868
  95.8 8.2 %copy-start.2 = (bf16[1,256,1024]{2,1,0:T(8,128)(2,1)S(1)}, bf16[1,256,1024]{2,1,0:T(8,128)(2,1)}, u32[]{:S(2)}) copy-start(bf16[1,256,1024]{2,1,0:T(8,128)(2,1)} %param.13) | copy-start | bytes 1572868
  95.8 8.3 %copy-start.5 = (s32[1,64]{1,0:T(1,128)S(1)}, s32[1,64]{1,0:T(1,128)}, u32[]{:S(2)}) copy-start(s32[1,64]{1,0:T(1,128)} %param.15) | copy-start | bytes 772
  95.8 23.1 %all-to-all-start.1 = ((f32[16,64,192]{2,1,0:T(8,128)}), f32[16,64,192]{2,1,0:T(8,128)S(1)}, u32[]{:S(2)}, u32[]{:S(2)}) async-start(f32[16,64,192]{2,1,0:T(8,128)} %bitcast.100), calls=%async_computation.1 | async-start | bytes 2097152 | tf_op jit(solution)/shard_map/all_to_all | solution.py:28
  120.1 17.6 %all-to-all-start.3 = ((bf16[16,64,384]{2,1,0:T(8,128)(2,1)}), bf16[16,64,384]{2,1,0:T(8,128)(2,1)S(1)}, u32[]{:S(2)}, u32[]{:S(2)}) async-start(bf16[16,64,384]{2,1,0:T(8,128)(2,1)} %broadcast_in_dim.89), calls=%async_computation.3 | async-start | bytes 1572864 | tf_op jit(solution)/shard_map/all_to_all | solution.py:35
  137.7 2.3 %copy-start.3 = (bf16[32,8,8,128]{3,2,1,0:T(8,128)(2,1)S(1)}, bf16[32,8,8,128]{3,2,1,0:T(8,128)(2,1)}, u32[]{:S(2)}) copy-start(bf16[32,8,8,128]{3,2,1,0:T(8,128)(2,1)} %copy.117) | copy-start | bytes 1572868
  137.8 0.9 copy-start
  144.6 19.2 %all-to-all-start.4 = ((f32[1,16,2,65,128]{4,2,3,0,1:T(2,128)}), f32[1,16,2,65,128]{4,2,3,0,1:T(2,128)S(1)}, u32[]{:S(2)}, u32[]{:S(2)}) async-start(f32[1,16,2,65,128]{4,2,3,0,1:T(2,128)} %maximum_maximum_fusion), calls=%async_computation.4 | async-start | bytes 2129920 | tf_op jit(solution)/shard_map/all_to_all | solution.py:108
Sparse Core Ops, SparseCore 0:
  9.2 43.0 all-gather.5
  54.1 37.5 all-gather.3
  93.5 39.2 all-gather.7
where the time goes:
time: 191 us; the launch traced here: 190 us
  waiting for transfers between devices  98 us (51%)
  starting transfers between devices  29.4 us (15%)
  local copies, waits for them, and re-layouts  19.3 us (10%)
  blocking collectives  14.8 us (8%)
  between operations  14.1 us (7%)
  other arithmetic  7.51 us (4%)
  matrix products  7.26 us (4%)
    all_gather x2, waiting for transfers between devices, shards(): lax.all_gather(part, 'col', axis=1, tiled=True)  56.3 us
    all_to_all x2, waiting for transfers between devices, row_gather(): return lax.all_to_all(copies, axis_name, 0, 0)  17.4 us
    all_to_all x1, blocking collectives, row_reduce(): received = lax.all_to_all(pieces, axis_name, 0, 0)  14.8 us
    all_to_all x2, waiting for transfers between devices, row_reduce(): received = lax.all_to_all(pieces, axis_name, 0, 0)  14.5 us
    all_to_all x2, starting transfers between devices, row_reduce(): received = lax.all_to_all(pieces, axis_name, 0, 0)  13.3 us
    all_to_all x2, starting transfers between devices, row_gather(): return lax.all_to_all(copies, axis_name, 0, 0)  12.1 us
    all_to_all x1, waiting for transfers between devices, shards(): gathered = lax.all_to_all(packed, 'row', 1, 1)  9.12 us
    unnamed x19, local copies, waits for them, and re-layouts  6.45 us
  transfers between devices with their start and end apart: 8, of which 6 were waited for; matrix products, arithmetic and copies ran while one was open for 14% of the time, Pallas kernels for 0%

commit v1 on v0

--- a/solution.py
+++ b/solution.py
@@ -8,6 +8,12 @@
 KEY_VALUE_HEADS = 8
 HEAD_SIZE = 128
 masked_score = -1e30
+
+
+def read_rails(u, row_axis):
+    top = jnp.stack([u for _ in range(lax.axis_size(row_axis))])
+    state_next = lax.all_to_all(top, row_axis, 0, 0)
+    return jnp.concatenate(state_next, axis=1)
 
 
 def ancestors(parents):
@@ -54,11 +60,7 @@
     half = w_qkv.shape[1] // 2
     halves = []
     for part in (w_qkv[:, :half], w_qkv[:, half:]):
-        partial_value = jnp.dot(
-            normed,
-            lax.all_gather(part, "col", axis=1, tiled=True),
-            preferred_element_type=jnp.float32,
-        )
+        partial_value = jnp.dot(normed, read_rails(part, "col"), preferred_element_type=jnp.float32)
         halves.append(row_reduce(partial_value, "row"))
     summed = jnp.concatenate(halves, axis=1).astype(jnp.bfloat16)
     projected_output = row_gather(summed, "row").transpose(1, 0, 2).reshape(rows_here, -1)

time: 191 us -> 239 us (1.25)
  waiting for transfers between devices: 98 us -> 141 us
  starting transfers between devices: 29.4 us -> 38 us
  local copies, waits for them, and re-layouts: 19.3 us -> 16.6 us
    all_to_all x0 -> x2, waiting for transfers between devices: none -> 80.1 us  [read_rails(): state_next = lax.all_to_all(top, row_axis, 0, 0)]
    all_gather x2 -> x0, waiting for transfers between devices: 56.3 us -> none  [shards(): lax.all_gather(part, 'col', axis=1, tiled=True)]
    all_to_all x2, waiting for transfers between devices: 14.5 us -> 33 us  [row_reduce(): received = lax.all_to_all(pieces, axis_name, 0, 0)]
    all_to_all x0 -> x2, starting transfers between devices: none -> 14.7 us  [read_rails(): state_next = lax.all_to_all(top, row_axis, 0, 0)]
    all_to_all x2, starting transfers between devices: 13.3 us -> 7.31 us  [row_reduce(): received = lax.all_to_all(pieces, axis_name, 0, 0)]
    reshape x4 -> x0, local copies, waits for them, and re-layouts: 4.12 us -> none  [row_reduce(): partial.reshape(rows, count, cols // count).transpose(1, 0, 2).astype(sent)]
    another operation x0 -> x2, local copies, waits for them, and re-layouts: none -> 2.61 us  [read_rails(): top = jnp.stack([u for _ in range(lax.axis_size(row_axis))])]
  transfers between devices with their start and end apart: 8 -> 8, of which waited for: 6 -> 7; matrix products, arithmetic and copies ran while one was open for 14% -> 8% of each run, Pallas kernels for 0% -> 0%
where the time goes in v1:
time: 239 us; the launch traced here: 238 us
  waiting for transfers between devices  141 us (59%)
  starting transfers between devices  38 us (16%)
  local copies, waits for them, and re-layouts  16.6 us (7%)
  blocking collectives  15.1 us (6%)
  between operations  14.4 us (6%)
  other arithmetic  6.85 us (3%)
  matrix products  6.49 us (3%)
    all_to_all x2, waiting for transfers between devices, read_rails(): state_next = lax.all_to_all(top, row_axis, 0, 0)  80.1 us
    all_to_all x2, waiting for transfers between devices, row_reduce(): received = lax.all_to_all(pieces, axis_name, 0, 0)  33 us
    all_to_all x2, waiting for transfers between devices, row_gather(): return lax.all_to_all(copies, axis_name, 0, 0)  17.4 us
    all_to_all x1, blocking collectives, row_reduce(): received = lax.all_to_all(pieces, axis_name, 0, 0)  15.1 us
    all_to_all x2, starting transfers between devices, read_rails(): state_next = lax.all_to_all(top, row_axis, 0, 0)  14.7 us
    all_to_all x2, starting transfers between devices, row_gather(): return lax.all_to_all(copies, axis_name, 0, 0)  11.8 us
    all_to_all x1, waiting for transfers between devices, shards(): gathered = lax.all_to_all(packed, 'row', 1, 1)  9.29 us
    all_to_all x2, starting transfers between devices, row_reduce(): received = lax.all_to_all(pieces, axis_name, 0, 0)  7.31 us
  transfers between devices with their start and end apart: 8, of which 7 were waited for; matrix products, arithmetic and copies ran while one was open for 8% of the time, Pallas kernels for 0%

profile of v1, /device:TPU:1, one launch (start us, length us, event | category | flops | bytes accessed | tf_op | source)
XLA Modules:
  0.0 238.0 jit_solution(10289085891021872338)
XLA Ops:
  6.5 0.9 fusion.35
  7.4 0.6 broadcast_in_dim.88
  8.0 7.6 %all-to-all-start = ((f32[16,1,64]{2,1,0:T(1,128)}), f32[16,1,64]{2,1,0:T(1,128)S(1)}, u32[]{:S(2)}, u32[]{:S(2)}) async-start(f32[16,1,64]{2,1,0:T(1,128)} %broadcast_in_dim.88), calls=%async_computation | async-start | bytes 16384 | tf_op jit(solution)/shard_map/all_to_all | solution.py:41
  15.6 1.1 fusion.62
  16.8 5.2 %all-to-all-done = f32[16,1,64]{2,1,0:T(1,128)S(1)} async-done(((f32[16,1,64]{2,1,0:T(1,128)}), f32[16,1,64]{2,1,0:T(1,128)S(1)}, u32[]{:S(2)}, u32[]{:S(2)}) %all-to-all-start) | async-done | bytes 4128 | tf_op jit(solution)/shard_map/all_to_all | solution.py:41
  22.0 1.3 stack.5
  23.3 10.6 %all-to-all-start.3 = ((bf16[16,256,192]{1,2,0:T(8,128)(2,1)}), bf16[16,256,192]{1,2,0:T(8,128)(2,1)S(1)}, u32[]{:S(2)}, u32[]{:S(2)}) async-start(bf16[16,256,192]{1,2,0:T(8,128)(2,1)} %stack.5), calls=%async_computation.3 | async-start | bytes 3145728 | tf_op jit(solution)/shard_map/all_to_all | solution.py:15
  34.0 38.4 %all-to-all-done.3 = bf16[16,256,192]{1,2,0:T(8,128)(2,1)S(1)} async-done(((bf16[16,256,192]{1,2,0:T(8,128)(2,1)}), bf16[16,256,192]{1,2,0:T(8,128)(2,1)S(1)}, u32[]{:S(2)}, u32[]{:S(2)}) %all-to-all-start.3) | async-done | bytes 1572896 | tf_op jit(solution)/shard_map/all_to_all | solution.py:15
  72.4 1.3 stack.4
  73.7 4.1 %all-to-all-start.1 = ((bf16[16,256,192]{1,2,0:T(8,128)(2,1)}), bf16[16,256,192]{1,2,0:T(8,128)(2,1)S(1)}, u32[]{:S(2)}, u32[]{:S(2)}) async-start(bf16[16,256,192]{1,2,0:T(8,128)(2,1)} %stack.4), calls=%async_computation.1 | async-start | bytes 3145728 | tf_op jit(solution)/shard_map/all_to_all | solution.py:15
  77.9 0.7 all-gather.2.cloned.1.call-update
  78.6 1.6 fusion.11
  80.2 41.7 %all-to-all-done.1 = bf16[16,256,192]{1,2,0:T(8,128)(2,1)S(1)} async-done(((bf16[16,256,192]{1,2,0:T(8,128)(2,1)}), bf16[16,256,192]{1,2,0:T(8,128)(2,1)S(1)}, u32[]{:S(2)}, u32[]{:S(2)}) %all-to-all-start.1) | async-done | bytes 1572896 | tf_op jit(solution)/shard_map/all_to_all | solution.py:15
  121.9 3.7 %all-to-all-start.4 = ((f32[16,64,192]{2,1,0:T(8,128)}), f32[16,64,192]{2,1,0:T(8,128)S(1)}, u32[]{:S(2)}, u32[]{:S(2)}) async-start(f32[16,64,192]{2,1,0:T(8,128)} %fusion.11), calls=%async_computation.4 | async-start | bytes 2097152 | tf_op jit(solution)/shard_map/all_to_all | solution.py:34
  125.5 1.6 fusion.8
  127.2 18.2 %all-to-all-done.4 = f32[16,64,192]{2,1,0:T(8,128)S(1)} async-done(((f32[16,64,192]{2,1,0:T(8,128)}), f32[16,64,192]{2,1,0:T(8,128)S(1)}, u32[]{:S(2)}, u32[]{:S(2)}) %all-to-all-start.4) | async-done | bytes 786464 | tf_op jit(solution)/shard_map/all_to_all | solution.py:34
  145.3 3.7 %all-to-all-start.2 = ((f32[16,64,192]{2,1,0:T(8,128)}), f32[16,64,192]{2,1,0:T(8,128)S(1)}, u32[]{:S(2)}, u32[]{:S(2)}) async-start(f32[16,64,192]{2,1,0:T(8,128)} %fusion.8), calls=%async_computation.2 | async-start | bytes 2097152 | tf_op jit(solution)/shard_map/all_to_all | solution.py:34
  149.7 0.9 copy.111
  150.7 0.1 fusion.42
  150.9 14.9 %all-to-all-done.2 = f32[16,64,192]{2,1,0:T(8,128)S(1)} async-done(((f32[16,64,192]{2,1,0:T(8,128)}), f32[16,64,192]{2,1,0:T(8,128)S(1)}, u32[]{:S(2)}, u32[]{:S(2)}) %all-to-all-start.2) | async-done | bytes 786464 | tf_op jit(solution)/shard_map/all_to_all | solution.py:34
  166.0 1.0 broadcast_in_dim.89
  167.0 4.3 %all-to-all-start.5 = ((bf16[16,64,384]{2,1,0:T(8,128)(2,1)}), bf16[16,64,384]{2,1,0:T(8,128)(2,1)S(1)}, u32[]{:S(2)}, u32[]{:S(2)}) async-start(bf16[16,64,384]{2,1,0:T(8,128)(2,1)} %broadcast_in_dim.89), calls=%async_computation.5 | async-start | bytes 1572864 | tf_op jit(solution)/shard_map/all_to_all | solution.py:41
  171.2 0.2 convolution_compare_fusion.5
  171.6 0.1 convolution_compare_fusion.3
  171.7 0.1 convolution_compare_fusion.2
  171.8 0.1 convolution_compare_fusion.1
  172.0 12.3 %all-to-all-done.5 = bf16[16,64,384]{2,1,0:T(8,128)(2,1)S(1)} async-done(((bf16[16,64,384]{2,1,0:T(8,128)(2,1)}), bf16[16,64,384]{2,1,0:T(8,128)(2,1)S(1)}, u32[]{:S(2)}, u32[]{:S(2)}) %all-to-all-start.5) | async-done | bytes 786464 | tf_op jit(solution)/shard_map/all_to_all | solution.py:41
  184.3 0.9 copy-done
  185.2 1.0 slice_bitcast_fusion.3
  186.2 0.4 squeeze.24
  186.5 0.6 bitcast_reduce_fusion
  187.2 0.7 fusion.22
  187.8 0.8 copy.89
  188.7 0.9 fusion.6
  189.6 1.5 maximum_maximum_fusion
  191.1 4.2 %all-to-all-start.6 = ((f32[1,16,2,65,128]{4,2,3,0,1:T(2,128)}), f32[1,16,2,65,128]{4,2,3,0,1:T(2,128)S(1)}, u32[]{:S(2)}, u32[]{:S(2)}) async-start(f32[1,16,2,65,128]{4,2,3,0,1:T(2,128)} %maximum_maximum_fusion), calls=%async_computation.6 | async-start | bytes 2129920 | tf_op jit(solution)/shard_map/all_to_all | solution.py:110
  195.3 0.1 fusion.21
  195.5 3.3 %copy.99 = bf16[4096,256]{1,0:T(8,128)(2,1)S(1)} copy(bf16[4096,256]{0,1:T(8,128)(2,1)} %bitcast.128) | data formatting | bytes 4194304 | tf_op jit(solution)/shard_map/dot_general | solution.py:148
  198.8 1.1 copy.113
  200.0 1.0 slice_bitcast_fusion
  201.2 0.2 fusion.63
  201.4 9.3 %all-to-all-done.6 = f32[1,16,2,65,128]{4,2,3,0,1:T(2,128)S(1)} async-done(((f32[1,16,2,65,128]{4,2,3,0,1:T(2,128)}), f32[1,16,2,65,128]{4,2,3,0,1:T(2,128)S(1)}, u32[]{:S(2)}, u32[]{:S(2)}) %all-to-all-start.6) | async-done | bytes 1064992 | tf_op jit(solution)/shard_map/all_to_all | solution.py:110
  210.7 1.0 copy.94
  211.9 2.2 fusion.24
  214.2 0.2 fusion.19
  214.5 0.8 fusion.14
  215.3 15.1 %all_to_all.41 = bf16[16,64,256]{2,1,0:T(8,128)(2,1)S(1)} all-to-all(bf16[16,64,256]{2,1,0:T(8,128)(2,1)S(1)} %fusion.14), channel_id=1, replica_groups=mesh['row'=16,'col'=16] {'row'}, dimensions={0} | all-to-all | bytes 1048576 | tf_op jit(solution)/shard_map/all_to_all | solution.py:34
  230.4 0.7 reduce_sum.93
  (40 shorter events, 1.5 us)
Async XLA Ops:
  8.0 13.9 %all-to-all-start = ((f32[16,1,64]{2,1,0:T(1,128)}), f32[16,1,64]{2,1,0:T(1,128)S(1)}, u32[]{:S(2)}, u32[]{:S(2)}) async-start(f32[16,1,64]{2,1,0:T(1,128)} %broadcast_in_dim.88), calls=%async_computation | async-start | bytes 16384 | tf_op jit(solution)/shard_map/all_to_all | solution.py:41
  23.3 49.1 %all-to-all-start.3 = ((bf16[16,256,192]{1,2,0:T(8,128)(2,1)}), bf16[16,256,192]{1,2,0:T(8,128)(2,1)S(1)}, u32[]{:S(2)}, u32[]{:S(2)}) async-start(bf16[16,256,192]{1,2,0:T(8,128)(2,1)} %stack.5), calls=%async_computation.3 | async-start | bytes 3145728 | tf_op jit(solution)/shard_map/all_to_all | solution.py:15
  34.0 44.6 %copy-start.6 = (bf16[256]{0:T(256)(128)(2,1)S(1)}, bf16[256]{0:T(256)(128)(2,1)}, u32[]{:S(2)}) copy-start(bf16[256]{0:T(256)(128)(2,1)} %param.9) | copy-start | bytes 1540
  34.0 44.6 %copy-start.4 = (bf16[64,256]{1,0:T(8,128)(2,1)S(1)}, bf16[64,256]{1,0:T(8,128)(2,1)}, u32[]{:S(2)}) copy-start(bf16[64,256]{1,0:T(8,128)(2,1)} %param.8) | copy-start | bytes 98308
  73.7 48.2 %all-to-all-start.1 = ((bf16[16,256,192]{1,2,0:T(8,128)(2,1)}), bf16[16,256,192]{1,2,0:T(8,128)(2,1)S(1)}, u32[]{:S(2)}, u32[]{:S(2)}) async-start(bf16[16,256,192]{1,2,0:T(8,128)(2,1)} %stack.4), calls=%async_computation.1 | async-start | bytes 3145728 | tf_op jit(solution)/shard_map/all_to_all | solution.py:15
  77.8 117.7 %all-gather.2.cloned.1.call-start = ((), (), s32[]{:S(2)}) async-start(), calls=%async_computation.8 | async-start | bytes 2228224 | tf_op jit(solution)/shard_map/all_gather | solution.py:150
  121.9 23.5 %all-to-all-start.4 = ((f32[16,64,192]{2,1,0:T(8,128)}), f32[16,64,192]{2,1,0:T(8,128)S(1)}, u32[]{:S(2)}, u32[]{:S(2)}) async-start(f32[16,64,192]{2,1,0:T(8,128)} %fusion.11), calls=%async_computation.4 | async-start | bytes 2097152 | tf_op jit(solution)/shard_map/all_to_all | solution.py:34
  127.2 22.5 %copy-start.1 = (bf16[1,256,1024]{2,1,0:T(8,128)(2,1)S(1)}, bf16[1,256,1024]{2,1,0:T(8,128)(2,1)}, u32[]{:S(2)}) copy-start(bf16[1,256,1024]{2,1,0:T(8,128)(2,1)} %param.12) | copy-start | bytes 1572868
  127.2 23.4 %copy-start.2 = (bf16[1,256,1024]{2,1,0:T(8,128)(2,1)S(1)}, bf16[1,256,1024]{2,1,0:T(8,128)(2,1)}, u32[]{:S(2)}) copy-start(bf16[1,256,1024]{2,1,0:T(8,128)(2,1)} %param.13) | copy-start | bytes 1572868
  127.2 23.5 %copy-start.5 = (s32[1,64]{1,0:T(1,128)S(1)}, s32[1,64]{1,0:T(1,128)}, u32[]{:S(2)}) copy-start(s32[1,64]{1,0:T(1,128)} %param.15) | copy-start | bytes 772
  145.3 20.5 %all-to-all-start.2 = ((f32[16,64,192]{2,1,0:T(8,128)}), f32[16,64,192]{2,1,0:T(8,128)S(1)}, u32[]{:S(2)}, u32[]{:S(2)}) async-start(f32[16,64,192]{2,1,0:T(8,128)} %fusion.8), calls=%async_computation.2 | async-start | bytes 2097152 | tf_op jit(solution)/shard_map/all_to_all | solution.py:34
  167.0 17.3 %all-to-all-start.5 = ((bf16[16,64,384]{2,1,0:T(8,128)(2,1)}), bf16[16,64,384]{2,1,0:T(8,128)(2,1)S(1)}, u32[]{:S(2)}, u32[]{:S(2)}) async-start(bf16[16,64,384]{2,1,0:T(8,128)(2,1)} %broadcast_in_dim.89), calls=%async_computation.5 | async-start | bytes 1572864 | tf_op jit(solution)/shard_map/all_to_all | solution.py:41
  184.2 2.3 copy-start.3
  184.3 0.9 copy-start
  191.1 19.6 %all-to-all-start.6 = ((f32[1,16,2,65,128]{4,2,3,0,1:T(2,128)}), f32[1,16,2,65,128]{4,2,3,0,1:T(2,128)S(1)}, u32[]{:S(2)}, u32[]{:S(2)}) async-start(f32[1,16,2,65,128]{4,2,3,0,1:T(2,128)} %maximum_maximum_fusion), calls=%async_computation.6 | async-start | bytes 2129920 | tf_op jit(solution)/shard_map/all_to_all | solution.py:110
Sparse Core Ops, SparseCore 0:
  80.4 54.4 all-gather.1
